TPU v7x, 32 devices: a whole 2x2x4 slice. The times are simulated.
32 devices in a mesh: leaf: 16 (over z, y, x), col: 2 (over core).
Axes of the slice: x: 2, y: 2, z: 4, core: 2. Of those that a mesh axis runs over, the one named last changes fastest.
Arguments:
- sources: bfloat16 [65536, 256], P('leaf', 'col'), may hold values from -6 to 6
- near_tiles: bfloat16 [256, 8, 256, 256], P('leaf', 'col'), may hold values from -0.125 to 0.125
- near_index: int32 [256, 8], P('leaf'), may hold values from 0 to 255, as said below
- near_count: int32 [256], P('leaf'), may hold values from 1 to 8, as said below
- leaf_basis: bfloat16 [256, 64, 256], P('leaf'), may hold values from -0.375 to 0.375
- leaf_coupling: bfloat16 [256, 64, 256], P('leaf'), may hold values from -0.375 to 0.375
- leaf_far: int32 [256, 4], P('leaf'), may hold values from 0 to 255, as said below
- up_leaf: bfloat16 [32, 64, 512], P('leaf'), may hold values from -0.25 to 0.25
- mid_coupling: bfloat16 [32, 64, 256], P('leaf'), may hold values from -0.375 to 0.375
- mid_far: int32 [32, 4], P('leaf'), may hold values from 0 to 31, as said below
- up_mid: bfloat16 [32, 64, 64], P('leaf'), may hold values from -0.75 to 0.75
- top_coupling: bfloat16 [4, 64, 256], replicated, may hold values from -0.4375 to 0.4375
Outputs:
- product: float32 [65536, 256], P('leaf', 'col')
Inputs may be any that keep to these rules, and one draw needn't show every extreme that they name: `near_index`: entry 0 of row i is i; the other 7 entries are distinct leaves j with j != i and |i - j| <= 8. Only the first near_count[i] slots of leaf i count; some leaf has all 8. `leaf_far`: row i holds 4 distinct leaves j != i with |i // 8 - j // 8| <= 1. `mid_far`: row a holds 4 distinct middle clusters b != a with |a // 8 - b // 8| <= 1.
All inputs are finite; a program needn't handle non-finite values.
Results may differ from a plain program's by a relative error of at most 0.01.
Values may be sent and summed in bfloat16 or wider, within the bound.
No kernel may reach another device: no remote copies, remote signals or barrier semaphores. Data moves between devices by JAX's collectives and lax.ppermute only.
A program may use at most 128 MiB of HBM per device.

v0:
```python
import jax
import jax.numpy as jnp
from jax import lax
from jax.sharding import PartitionSpec as P

CHILD = 8
FAR = 4


def padded(x, sides, width):
    for axis, dim in sides:
        size, length = (lax.axis_size(axis), x.shape[dim])
        up = [(i, (i + 1) % size) for i in range(size - 1)]
        down = [(j, i) for i, j in up]
        last = lax.slice_in_dim(x, length - width, length, axis=dim)
        first = lax.slice_in_dim(x, 0, width, axis=dim)
        before = lax.ppermute(last, axis, up)
        after = lax.ppermute(first, axis, down)
        x = jnp.concatenate([before, x, after], axis=dim)
    return x


def shards(
    sources,
    near_tiles,
    near_index,
    near_count,
    leaf_basis,
    leaf_coupling,
    leaf_far,
    up_leaf,
    mid_coupling,
    mid_far,
    up_mid,
    top_coupling,
):
    f32 = jnp.float32
    bf16 = jnp.bfloat16
    leaf_count = leaf_basis.shape[0]
    rank_size = leaf_basis.shape[1]
    leaf_size = leaf_basis.shape[2]
    col_count = sources.shape[1]
    mid_count = leaf_count // CHILD
    total_top = top_coupling.shape[0]
    device = lax.axis_index("leaf")
    first_leaf = device * leaf_count
    first_mid = device * mid_count
    window = padded(sources, (("leaf", 0),), CHILD * leaf_size)
    near_local = near_index - (first_leaf - CHILD)
    all_tiles = lax.all_gather(near_tiles, "col", axis=1, tiled=True)
    slot_count = all_tiles.shape[1]
    blocks = window.reshape(-1, leaf_size, window.shape[1])
    picked = blocks[near_local]
    live_mask = jnp.arange(slot_count)[None, :] < near_count[:, None]
    picked = jnp.where(live_mask[:, :, None, None], picked, jnp.zeros((), bf16))
    result = jnp.einsum("lsij,lsjc->lic", all_tiles, picked, preferred_element_type=f32)
    near_part = result.reshape(leaf_count * leaf_size, window.shape[1])
    leaf_blocks = sources.reshape(leaf_count, leaf_size, col_count)
    leaf_coef = jnp.einsum(
        "lrk,lkc->lrc", leaf_basis, leaf_blocks, preferred_element_type=f32
    ).astype(bf16)
    mid_coef = jnp.einsum(
        "qrk,qkc->qrc",
        up_leaf,
        leaf_coef.reshape(mid_count, CHILD * rank_size, col_count),
        preferred_element_type=f32,
    ).astype(bf16)
    mid_lift = jnp.einsum("qrs,qsc->qrc", up_mid, mid_coef, preferred_element_type=f32).astype(bf16)
    parent = (first_mid + jnp.arange(mid_count)) // CHILD
    mid_flat = mid_far.reshape(-1)
    top_range = jnp.arange(total_top)
    coef_piece = lax.all_gather(mid_coef, "leaf", axis=0, tiled=True)
    lift_piece = lax.all_gather(mid_lift, "leaf", axis=0, tiled=True)
    global_ids = jnp.arange(coef_piece.shape[0])
    group_map = (top_range[:, None] == (global_ids // CHILD)[None, :]).astype(bf16)
    top_total = jnp.einsum("pk,krc->prc", group_map, lift_piece, preferred_element_type=f32)
    global_ids = jnp.arange(coef_piece.shape[0])
    pick_map = (mid_flat[:, None] == global_ids[None, :]).astype(bf16)
    mid_picked = jnp.einsum("ik,krc->irc", pick_map, coef_piece, preferred_element_type=f32)
    top_coef = top_total.astype(bf16)
    parent_rows = top_coupling[parent]
    keep_mask = top_range[None, :] != parent[:, None]
    stacked = jnp.where(keep_mask[:, :, None, None], top_coef[None], jnp.zeros((), bf16))
    top_field = jnp.einsum(
        "qrk,qkc->qrc",
        parent_rows,
        stacked.reshape(mid_count, total_top * rank_size, col_count),
        preferred_element_type=f32,
    ).astype(bf16)
    mid_chosen = mid_picked.astype(bf16).reshape(mid_count, FAR * rank_size, col_count)
    mid_field = (
        jnp.einsum("qrk,qkc->qrc", mid_coupling, mid_chosen, preferred_element_type=f32)
        + jnp.einsum("qrs,qrc->qsc", up_mid, top_field, preferred_element_type=f32)
    ).astype(bf16)
    leaf_window = padded(leaf_coef, (("leaf", 0),), CHILD)
    far_local = leaf_far - (first_leaf - CHILD)
    leaf_chosen = leaf_window[far_local].reshape(leaf_count, FAR * rank_size, col_count)
    down_part = jnp.einsum("qrs,qrc->qsc", up_leaf, mid_field, preferred_element_type=f32).reshape(
        leaf_count, rank_size, col_count
    )
    leaf_field = (
        jnp.einsum("lrk,lkc->lrc", leaf_coupling, leaf_chosen, preferred_element_type=f32)
        + down_part
    ).astype(bf16)
    far_part = jnp.einsum(
        "lrk,lrc->lkc", leaf_basis, leaf_field, preferred_element_type=f32
    ).reshape(leaf_count * leaf_size, col_count)
    return near_part + far_part


def solution(mesh):
    return jax.shard_map(
        shards,
        mesh=mesh,
        in_specs=(
            P("leaf", "col"),
            P("leaf", "col", None, None),
            P("leaf", None),
            P("leaf"),
            P("leaf", None, None),
            P("leaf", None, None),
            P("leaf", None),
            P("leaf", None, None),
            P("leaf", None, None),
            P("leaf", None),
            P("leaf", None, None),
            P(),
        ),
        out_specs=P("leaf", "col"),
        check_vma=False,
    )
```

profile of v0, /device:TPU:0, one launch (start us, length us, event | category | flops | bytes accessed | tf_op | source)
XLA Modules:
  0.0 168.7 jit_solution(13844385451105794318)
XLA Ops:
  6.5 0.7 all-gather.2.cloned.1.call-update
  7.3 0.0 copy-start.9
  7.3 0.0 copy-start.4
  7.3 0.0 copy-start.6
  7.3 0.0 copy-start.11
  7.3 0.0 copy-start.7
  7.3 0.0 copy-start.10
  7.3 0.2 copy-done
  7.6 0.3 copy-done.1
  7.9 0.3 convolution_convert_fusion
  8.3 4.9 %collective-permute-start.2 = (bf16[8,64,128]{2,1,0:T(8,128)(2,1)S(1)}, bf16[8,64,128]{2,1,0:T(8,128)(2,1)S(1)}, u32[]{:S(2)}, u32[]{:S(2)}) collective-permute-start(bf16[8,64,128]{2,1,0:T(8,128)(2,1)S(1)} %get-tuple-element.7), channel_id=1, source_target_pairs={{0,2},{2,4},{4,6},{6,8},{8,10},{10,12},{12,14},{14,16},{16,18},{18... | collective-permute-start | bytes 393224 | tf_op jit(solution)/shard_map/ppermute | solution.py:17
  13.2 1.3 collective-permute-start.3
  14.5 1.1 fusion.33
  15.5 5.4 %collective-permute-start = (bf16[2048,128]{1,0:T(8,128)(2,1)}, bf16[2048,128]{1,0:T(8,128)(2,1)}, u32[]{:S(2)}, u32[]{:S(2)}) collective-permute-start(bf16[2048,128]{1,0:T(8,128)(2,1)} %get-tuple-element.5), channel_id=1, source_target_pairs={{0,2},{2,4},{4,6},{6,8},{8,10},{10,12},{12,14},{14,16},{16,18},{18... | collective-permute-start | bytes 1572872 | tf_op jit(solution)/shard_map/ppermute | solution.py:17
  20.9 1.3 collective-permute-start.1
  22.2 0.1 copy.27
  22.3 0.1 reshape.160
  22.4 0.2 convolution_convert_fusion.5
  22.6 0.1 fusion.12
  22.7 0.0 copy-start.3
  22.7 57.8 %all_gather.11 = bf16[32,64,128]{2,1,0:T(8,128)(2,1)S(1)} all-gather(bf16[2,64,128]{2,1,0:T(8,128)(2,1)S(1)} %fusion.12), channel_id=1, replica_groups=mesh['leaf'=16,'col'=2] {'leaf'}, dimensions={0}, use_global_device_ids=true | all-gather | bytes 557056 | tf_op jit(solution)/shard_map/all_gather | solution.py:73
  80.5 0.4 convolution_convert_fusion.2
  80.9 0.1 iota_compare_fusion.3
  81.0 0.1 broadcast_in_dim.59
  81.1 0.1 broadcast_in_dim.60
  81.2 0.1 eq.28
  81.3 38.7 %all_gather.10 = bf16[32,64,128]{2,1,0:T(8,128)(2,1)S(1)} all-gather(bf16[2,64,128]{2,1,0:T(8,128)(2,1)S(1)} %bitcast.59), channel_id=1, replica_groups=mesh['leaf'=16,'col'=2] {'leaf'}, dimensions={0}, use_global_device_ids=true | all-gather | bytes 557056 | tf_op jit(solution)/shard_map/all_gather | solution.py:72
  119.9 0.4 convolution_convert_fusion.1
  120.4 0.6 gather_fusion.2
  121.0 0.1 iota_compare_fusion
  121.1 0.4 fusion.11
  121.5 0.0 copy-done.5
  121.5 0.4 convolution_bitcast_fusion.1
  121.9 0.1 copy.25
  122.0 0.1 reshape.152
  122.1 0.2 copy.33
  122.3 0.0 collective-permute-done.2
  122.3 0.0 collective-permute-done.3
  122.3 1.0 pad_maximum_fusion.1
  123.3 0.7 gather_fusion.1
  124.0 1.9 %fusion.9 = f32[16,128,256]{2,1,0:T(8,128)} fusion(bf16[16,64,256]{2,1,0:T(8,128)(2,1)S(1)} %copy-done, f32[16,64,128]{2,1,0:T(8,128)S(1)} %bitcast.57, bf16[16,64,256]{2,1,0:T(8,128)(2,1)S(1)} %copy-done.3, bf16[16,256,128]{2,1,0:T(8,128)(2,1)S(1)} %bitcast.56), kind=kOutput, calls=%fused_computation.15 | convolution fusion | flops 134479872 | bytes 4718592 | tf_op jit(solution)/shard_map/lrk,lrc->lkc/dot_general | solution.py:105
  126.0 0.0 collective-permute-done
  126.0 0.0 collective-permute-done.1
  126.0 1.7 pad_maximum_fusion
  127.6 6.6 %gather_fusion = bf16[128,256,128]{2,1,0:T(8,128)(2,1)} fusion(bf16[32,256,128]{2,1,0:T(8,128)(2,1)S(1)} %bitcast.52, s32[1024]{0:T(1024)S(1)} %pad_clamp_fusion.2), kind=kCustom, calls=%fused_computation | custom fusion | bytes 16777728 | tf_op jit(solution)/shard_map/gather | solution.py:53
  134.2 12.1 %copy.26 = bf16[128,256,128]{1,2,0:T(8,128)(2,1)} copy(bf16[128,256,128]{2,1,0:T(8,128)(2,1)} %gather_fusion) | data formatting | bytes 16777216 | tf_op jit(solution)/shard_map/gather | solution.py:53
  146.3 12.7 %fusion.4 = f32[16,256,128]{1,2,0:T(8,128)} fusion(f32[16,128,256]{2,1,0:T(8,128)S(1)} %copy-done.2, bf16[16,8,256,256]{3,2,1,0:T(8,128)(2,1)} %all-gather.2.cloned.1.call-done, bf16[16,8,256,128]{2,3,1,0:T(8,128)(2,1)} %bitcast.54, pred[16,8]{1,0:T(8,128)(4,1)S(1)} %iota_compare_fusion), kind=kOutput, calls=%fused_computation.9 | convolution fusion | flops 2152202240 | bytes 29360256 | tf_op jit(solution)/shard_map/lsij,lsjc->lic/dot_general | solution.py:56
  159.0 2.9 %copy.34 = f32[16,256,128]{2,1,0:T(8,128)} copy(f32[16,256,128]{1,2,0:T(8,128)} %fusion.4) | data formatting | bytes 4194304 | tf_op jit(solution)/shard_map/add | solution.py:108
  (27 shorter events, 0.2 us)
Async XLA Ops:
  6.5 1.0 copy-start
  6.5 1.4 copy-start.1
  6.5 139.8 %all-gather.2.cloned.1.call-start = ((), (), s32[]{:S(2)}) async-start(), calls=%async_computation | async-start | bytes 25165824 | tf_op jit(solution)/shard_map/all_gather | solution.py:50
  7.3 14.9 %copy-start.9 = (s32[16,4]{0,1:T(4,128)S(1)}, s32[16,4]{0,1:T(4,128)}, u32[]{:S(2)}) copy-start(s32[16,4]{0,1:T(4,128)} %param.18) | copy-start | bytes 772
  7.3 15.1 %copy-start.4 = (bf16[2,64,512]{2,1,0:T(8,128)(2,1)S(1)}, bf16[2,64,512]{2,1,0:T(8,128)(2,1)}, u32[]{:S(2)}) copy-start(bf16[2,64,512]{2,1,0:T(8,128)(2,1)} %param.19) | copy-start | bytes 393220
  7.3 15.3 %copy-start.6 = (bf16[2,64,64]{2,1,0:T(8,128)(2,1)S(1)}, bf16[2,64,64]{2,1,0:T(8,128)(2,1)}, u32[]{:S(2)}) copy-start(bf16[2,64,64]{2,1,0:T(8,128)(2,1)} %param.22) | copy-start | bytes 49156
  7.3 73.9 %copy-start.11 = (s32[2,4]{1,0:T(2,128)S(1)}, s32[2,4]{1,0:T(2,128)}, u32[]{:S(2)}) copy-start(s32[2,4]{1,0:T(2,128)} %param.21) | copy-start | bytes 100
  7.3 113.1 %copy-start.7 = (bf16[4,64,256]{2,1,0:T(8,128)(2,1)S(1)}, bf16[4,64,256]{2,1,0:T(8,128)(2,1)}, u32[]{:S(2)}) copy-start(bf16[4,64,256]{2,1,0:T(8,128)(2,1)} %param.23) | copy-start | bytes 393220
  7.3 113.7 %copy-start.10 = (s32[16]{0:T(128)S(1)}, s32[16]{0:T(128)}, u32[]{:S(2)}) copy-start(s32[16]{0:T(128)} %param.15) | copy-start | bytes 196
  7.3 113.7 %copy-start.8 = (s32[16,8]{0,1:T(8,128)S(1)}, s32[16,8]{0,1:T(8,128)}, u32[]{:S(2)}) copy-start(s32[16,8]{0,1:T(8,128)} %param.14) | copy-start | bytes 1540
  7.3 114.1 %copy-start.5 = (bf16[2,64,256]{2,1,0:T(8,128)(2,1)S(1)}, bf16[2,64,256]{2,1,0:T(8,128)(2,1)}, u32[]{:S(2)}) copy-start(bf16[2,64,256]{2,1,0:T(8,128)(2,1)} %param.20) | copy-start | bytes 196612
  8.3 114.0 %collective-permute-start.2 = (bf16[8,64,128]{2,1,0:T(8,128)(2,1)S(1)}, bf16[8,64,128]{2,1,0:T(8,128)(2,1)S(1)}, u32[]{:S(2)}, u32[]{:S(2)}) collective-permute-start(bf16[8,64,128]{2,1,0:T(8,128)(2,1)S(1)} %get-tuple-element.7), channel_id=1, source_target_pairs={{0,2},{2,4},{4,6},{6,8},{8,10},{10,12},{12,14},{14,16},{16,18},{18... | collective-permute-start | bytes 393224 | tf_op jit(solution)/shard_map/ppermute | solution.py:17
  13.2 109.1 %collective-permute-start.3 = (bf16[8,64,128]{2,1,0:T(8,128)(2,1)S(1)}, bf16[8,64,128]{2,1,0:T(8,128)(2,1)}, u32[]{:S(2)}, u32[]{:S(2)}) collective-permute-start(bf16[8,64,128]{2,1,0:T(8,128)(2,1)S(1)} %get-tuple-element.8), channel_id=1, source_target_pairs={{2,0},{4,2},{6,4},{8,6},{10,8},{12,10},{14,12},{16,14},{18,16},{20... | collective-permute-start | bytes 393224 | tf_op jit(solution)/shard_map/ppermute | solution.py:18
  15.5 110.4 %collective-permute-start = (bf16[2048,128]{1,0:T(8,128)(2,1)}, bf16[2048,128]{1,0:T(8,128)(2,1)}, u32[]{:S(2)}, u32[]{:S(2)}) collective-permute-start(bf16[2048,128]{1,0:T(8,128)(2,1)} %get-tuple-element.5), channel_id=1, source_target_pairs={{0,2},{2,4},{4,6},{6,8},{8,10},{10,12},{12,14},{14,16},{16,18},{18... | collective-permute-start | bytes 1572872 | tf_op jit(solution)/shard_map/ppermute | solution.py:17
  20.9 105.1 %collective-permute-start.1 = (bf16[2048,128]{1,0:T(8,128)(2,1)}, bf16[2048,128]{1,0:T(8,128)(2,1)}, u32[]{:S(2)}, u32[]{:S(2)}) collective-permute-start(bf16[2048,128]{1,0:T(8,128)(2,1)} %get-tuple-element.6), channel_id=1, source_target_pairs={{2,0},{4,2},{6,4},{8,6},{10,8},{12,10},{14,12},{16,14},{18,16},{20... | collective-permute-start | bytes 1572872 | tf_op jit(solution)/shard_map/ppermute | solution.py:18
  22.7 101.3 %copy-start.3 = (bf16[16,64,256]{2,1,0:T(8,128)(2,1)S(1)}, bf16[16,64,256]{2,1,0:T(8,128)(2,1)}, u32[]{:S(2)}) copy-start(bf16[16,64,256]{2,1,0:T(8,128)(2,1)} %param.17) | copy-start | bytes 1572868
  134.2 12.1 %copy-start.2 = (f32[16,128,256]{2,1,0:T(8,128)S(1)}, f32[16,128,256]{2,1,0:T(8,128)}, u32[]{:S(2)}) copy-start(f32[16,128,256]{2,1,0:T(8,128)} %fusion.9) | copy-start | bytes 6291460
Sparse Core Ops, SparseCore 0:
  8.9 32.7 all-gather.1
where the time goes:
time: 169 us
  blocking collectives  96.5 us (57%)
  local copies, waits for them, and re-layouts  25.4 us (15%)
  matrix products  16.8 us (10%)
  between operations  13.7 us (8%)
  starting transfers between devices  12.8 us (8%)
  other arithmetic  2.82 us (2%)
    all_gather x1, blocking collectives, shards(): lift_piece = lax.all_gather(mid_lift, 'leaf', axis=0, tiled=True)  57.8 us
    all_gather x1, blocking collectives, shards(): coef_piece = lax.all_gather(mid_coef, 'leaf', axis=0, tiled=True)  38.7 us
    gather x2, local copies, waits for them, and re-layouts, shards(): picked = blocks[near_local]  18.7 us
    dot_general x1, matrix products, shards(): jnp.einsum('lsij,lsjc->lic', all_tiles, picked, preferred_element_type=f32)  12.7 us
    ppermute x2, starting transfers between devices, padded(): before = lax.ppermute(last, axis, up)  10.2 us
  transfers between devices with their start and end apart: 5, of which 0 were waited for; matrix products, arithmetic and copies ran while one was open for 17% of the time, Pallas kernels for 0%

commit v1 on v0

--- a/solution.py
+++ b/solution.py
@@ -5,6 +5,22 @@
 
 CHILD = 8
 FAR = 4
+
+
+def ring_product(x, axis, dim, term):
+    devices, here, rows = (lax.axis_size(axis), lax.axis_index(axis), x.shape[dim])
+    upward = [(i, (i + 1) % devices) for i in range(devices)]
+    behind = [(i, (i - 1) % devices) for i in range(devices)]
+    halfway = devices // 2
+    from_left = from_right = x
+    total = term(x, here * rows)
+    for step in range(1, halfway + 1):
+        from_left = lax.ppermute(from_left, axis, upward)
+        if step < devices - halfway:
+            from_right = lax.ppermute(from_right, axis, behind)
+            total = total + term(from_right, (here + step) % devices * rows)
+        total = total + term(from_left, (here - step) % devices * rows)
+    return total
 
 
 def padded(x, sides, width):
@@ -70,10 +86,19 @@
     mid_flat = mid_far.reshape(-1)
     top_range = jnp.arange(total_top)
     coef_piece = lax.all_gather(mid_coef, "leaf", axis=0, tiled=True)
-    lift_piece = lax.all_gather(mid_lift, "leaf", axis=0, tiled=True)
     global_ids = jnp.arange(coef_piece.shape[0])
     group_map = (top_range[:, None] == (global_ids // CHILD)[None, :]).astype(bf16)
-    top_total = jnp.einsum("pk,krc->prc", group_map, lift_piece, preferred_element_type=f32)
+    top_total = ring_product(
+        mid_lift,
+        "leaf",
+        0,
+        lambda part, at: jnp.einsum(
+            "pk,krc->prc",
+            lax.dynamic_slice_in_dim(group_map, at, part.shape[0], axis=1),
+            part,
+            preferred_element_type=f32,
+        ),
+    )
     global_ids = jnp.arange(coef_piece.shape[0])
     pick_map = (mid_flat[:, None] == global_ids[None, :]).astype(bf16)
     mid_picked = jnp.einsum("ik,krc->irc", pick_map, coef_piece, preferred_element_type=f32)

time: 169 us -> 195 us (1.15)
  blocking collectives: 96.5 us -> 49.3 us
  waiting for transfers between devices: 0.72 us -> 33.3 us
  starting transfers between devices: 12.8 us -> 42.8 us
  matrix products: 16.8 us -> 24.1 us
    all_gather x1 -> x0, blocking collectives: 57.8 us -> none  [shards(): lift_piece = lax.all_gather(mid_lift, 'leaf', axis=0, tiled=True)]
    ppermute x0 -> x15, starting transfers between devices: none -> 33.5 us  [the longest x7 26.7 us: ring_product(): from_right = lax.ppermute(from_right, axis, behind)]
    ppermute x0 -> x15, waiting for transfers between devices: none -> 32.6 us  [the longest x8 24.1 us: ring_product(): from_left = lax.ppermute(from_left, axis, upward)]
    all_gather x1, blocking collectives: 38.7 us -> 49.3 us  [shards(): coef_piece = lax.all_gather(mid_coef, 'leaf', axis=0, tiled=True)]
    dot_general x1 -> x16, matrix products: 0.4 us -> 6.03 us  [shards(): jnp.einsum('pk,krc->prc', lax.dynamic_slice_in_dim(group_map, at, part.sh...]
    ppermute x2, starting transfers between devices: 10.2 us -> 6.63 us  [padded(): before = lax.ppermute(last, axis, up)]
  transfers between devices with their start and end apart: 5 -> 20, of which waited for: 0 -> 9; matrix products, arithmetic and copies ran while one was open for 17% -> 20% of each run, Pallas kernels for 0% -> 0%
where the time goes in v1:
time: 195 us; the launch traced here: 194 us
  blocking collectives  49.3 us (25%)
  starting transfers between devices  42.8 us (22%)
  waiting for transfers between devices  33.3 us (17%)
  local copies, waits for them, and re-layouts  27.2 us (14%)
  matrix products  24.1 us (12%)
  between operations  14.1 us (7%)
  other arithmetic  2.97 us (2%)
    all_gather x1, blocking collectives, shards(): coef_piece = lax.all_gather(mid_coef, 'leaf', axis=0, tiled=True)  49.3 us
    ppermute x7, starting transfers between devices, ring_product(): from_right = lax.ppermute(from_right, axis, behind)  26.7 us
    ppermute x8, waiting for transfers between devices, ring_product(): from_left = lax.ppermute(from_left, axis, upward)  24.1 us
    gather x2, local copies, waits for them, and re-layouts, shards(): picked = blocks[near_local]  18.7 us
    dot_general x1, matrix products, shards(): jnp.einsum('lsij,lsjc->lic', all_tiles, picked, preferred_element_type=f32)  12.7 us
    ppermute x7, waiting for transfers between devices, ring_product(): from_right = lax.ppermute(from_right, axis, behind)  8.5 us
    ppermute x8, starting transfers between devices, ring_product(): from_left = lax.ppermute(from_left, axis, upward)  6.83 us
    ppermute x2, starting transfers between devices, padded(): before = lax.ppermute(last, axis, up)  6.63 us
  transfers between devices with their start and end apart: 20, of which 9 were waited for; matrix products, arithmetic and copies ran while one was open for 20% of the time, Pallas kernels for 0%

profile of v1, /device:TPU:0, one launch (start us, length us, event | category | flops | bytes accessed | tf_op | source)
XLA Modules:
  0.0 193.8 jit_solution(1537536714810398697)
XLA Ops:
  6.6 0.7 all-gather.2.cloned.1.call-update
  7.3 0.3 copy-done
  7.6 0.3 copy-done.1
  7.9 0.3 convolution_convert_fusion
  8.6 7.0 %collective-permute-start.4 = (bf16[2,64,128]{2,1,0:T(8,128)(2,1)S(1)}, bf16[2,64,128]{2,1,0:T(8,128)(2,1)S(1)}, u32[]{:S(2)}, u32[]{:S(2)}) collective-permute-start(bf16[2,64,128]{2,1,0:T(8,128)(2,1)S(1)} %fusion.19), channel_id=1, source_target_pairs={{0,30},{2,0},{4,2},{6,4},{8,6},{10,8},{12,10},{14,12},{16,14},{18,... | collective-permute-start | bytes 98312 | tf_op jit(solution)/shard_map/ppermute | solution.py:20
  15.6 1.3 collective-permute-start.2
  16.9 1.3 collective-permute-start.3
  18.2 1.1 fusion.91
  19.2 5.3 %collective-permute-start = (bf16[2048,128]{1,0:T(8,128)(2,1)}, bf16[2048,128]{1,0:T(8,128)(2,1)}, u32[]{:S(2)}, u32[]{:S(2)}) collective-permute-start(bf16[2048,128]{1,0:T(8,128)(2,1)} %get-tuple-element.5), channel_id=1, source_target_pairs={{0,2},{2,4},{4,6},{6,8},{8,10},{10,12},{12,14},{14,16},{16,18},{18... | collective-permute-start | bytes 1572872 | tf_op jit(solution)/shard_map/ppermute | solution.py:33
  25.5 49.3 %all_gather.7 = bf16[32,64,128]{2,1,0:T(8,128)(2,1)S(1)} all-gather(bf16[2,64,128]{2,1,0:T(8,128)(2,1)S(1)} %bitcast.104), channel_id=1, replica_groups=mesh['leaf'=16,'col'=2] {'leaf'}, dimensions={0}, use_global_device_ids=true | all-gather | bytes 557056 | tf_op jit(solution)/shard_map/all_gather | solution.py:88
  74.9 0.4 convolution_convert_fusion.1
  75.6 0.7 broadcast_in_dim.60
  76.3 0.7 copy.61
  76.9 1.2 gather_fusion.2
  78.1 1.3 collective-permute-start.1
  79.4 2.7 %collective-permute-start.7 = (bf16[2,64,128]{2,1,0:T(8,128)(2,1)S(1)}, bf16[2,64,128]{2,1,0:T(8,128)(2,1)S(1)}, u32[]{:S(2)}, u32[]{:S(2)}) collective-permute-start(bf16[2,64,128]{2,1,0:T(8,128)(2,1)S(1)} %collective-permute-done.5), channel_id=1, source_target_pairs={{0,2},{2,4},{4,6},{6,8},{8,10},{10,12},{12,14},{14,16},{16,18},{18... | collective-permute-start | bytes 98312 | tf_op jit(solution)/shard_map/ppermute | solution.py:18
  82.6 4.5 %collective-permute-done.7 = bf16[2,64,128]{2,1,0:T(8,128)(2,1)S(1)} collective-permute-done((bf16[2,64,128]{2,1,0:T(8,128)(2,1)S(1)}, bf16[2,64,128]{2,1,0:T(8,128)(2,1)S(1)}, u32[]{:S(2)}, u32[]{:S(2)}) %collective-permute-start.7) | collective-permute-done | bytes 32800 | tf_op jit(solution)/shard_map/ppermute | solution.py:18
  87.1 1.3 collective-permute-start.6
  88.7 3.1 %collective-permute-done.6 = bf16[2,64,128]{2,1,0:T(8,128)(2,1)S(1)} collective-permute-done((bf16[2,64,128]{2,1,0:T(8,128)(2,1)S(1)}, bf16[2,64,128]{2,1,0:T(8,128)(2,1)S(1)}, u32[]{:S(2)}, u32[]{:S(2)}) %collective-permute-start.6) | collective-permute-done | bytes 32800 | tf_op jit(solution)/shard_map/ppermute | solution.py:20
  91.8 3.4 %collective-permute-start.9 = (bf16[2,64,128]{2,1,0:T(8,128)(2,1)S(1)}, bf16[2,64,128]{2,1,0:T(8,128)(2,1)S(1)}, u32[]{:S(2)}, u32[]{:S(2)}) collective-permute-start(bf16[2,64,128]{2,1,0:T(8,128)(2,1)S(1)} %collective-permute-done.7), channel_id=1, source_target_pairs={{0,2},{2,4},{4,6},{6,8},{8,10},{10,12},{12,14},{14,16},{16,18},{18... | collective-permute-start | bytes 98312 | tf_op jit(solution)/shard_map/ppermute | solution.py:18
  95.4 3.9 %collective-permute-done.9 = bf16[2,64,128]{2,1,0:T(8,128)(2,1)S(1)} collective-permute-done((bf16[2,64,128]{2,1,0:T(8,128)(2,1)S(1)}, bf16[2,64,128]{2,1,0:T(8,128)(2,1)S(1)}, u32[]{:S(2)}, u32[]{:S(2)}) %collective-permute-start.9) | collective-permute-done | bytes 32800 | tf_op jit(solution)/shard_map/ppermute | solution.py:18
  99.3 0.6 collective-permute-start.8
  100.1 3.1 %collective-permute-done.8 = bf16[2,64,128]{2,1,0:T(8,128)(2,1)S(1)} collective-permute-done((bf16[2,64,128]{2,1,0:T(8,128)(2,1)S(1)}, bf16[2,64,128]{2,1,0:T(8,128)(2,1)S(1)}, u32[]{:S(2)}, u32[]{:S(2)}) %collective-permute-start.8) | collective-permute-done | bytes 32800 | tf_op jit(solution)/shard_map/ppermute | solution.py:20
  103.2 0.7 collective-permute-start.11
  104.1 6.7 %collective-permute-done.11 = bf16[2,64,128]{2,1,0:T(8,128)(2,1)} collective-permute-done((bf16[2,64,128]{2,1,0:T(8,128)(2,1)S(1)}, bf16[2,64,128]{2,1,0:T(8,128)(2,1)}, u32[]{:S(2)}, u32[]{:S(2)}) %collective-permute-start.11) | collective-permute-done | bytes 32800 | tf_op jit(solution)/shard_map/ppermute | solution.py:18
  110.8 0.8 collective-permute-start.10
  111.6 1.0 fusion.39
  112.6 2.3 %collective-permute-done.10 = bf16[2,64,128]{2,1,0:T(8,128)(2,1)} collective-permute-done((bf16[2,64,128]{2,1,0:T(8,128)(2,1)S(1)}, bf16[2,64,128]{2,1,0:T(8,128)(2,1)}, u32[]{:S(2)}, u32[]{:S(2)}) %collective-permute-start.10) | collective-permute-done | bytes 32800 | tf_op jit(solution)/shard_map/ppermute | solution.py:20
  114.8 1.0 fusion.13
  115.9 5.7 %collective-permute-start.12 = (bf16[2,64,128]{2,1,0:T(8,128)(2,1)}, bf16[2,64,128]{2,1,0:T(8,128)(2,1)S(1)}, u32[]{:S(2)}, u32[]{:S(2)}) collective-permute-start(bf16[2,64,128]{2,1,0:T(8,128)(2,1)} %collective-permute-done.10), channel_id=1, source_target_pairs={{0,30},{2,0},{4,2},{6,4},{8,6},{10,8},{12,10},{14,12},{16,14},{18,... | collective-permute-start | bytes 98312 | tf_op jit(solution)/shard_map/ppermute | solution.py:20
  121.5 1.0 pad_maximum_fusion.1
  122.6 0.7 gather_fusion.1
  123.4 5.8 %collective-permute-start.14 = (bf16[2,64,128]{2,1,0:T(8,128)(2,1)S(1)}, bf16[2,64,128]{2,1,0:T(8,128)(2,1)S(1)}, u32[]{:S(2)}, u32[]{:S(2)}) collective-permute-start(bf16[2,64,128]{2,1,0:T(8,128)(2,1)S(1)} %collective-permute-done.12), channel_id=1, source_target_pairs={{0,30},{2,0},{4,2},{6,4},{8,6},{10,8},{12,10},{14,12},{16,14},{18,... | collective-permute-start | bytes 98312 | tf_op jit(solution)/shard_map/ppermute | solution.py:20
  129.3 1.0 fusion.36
  130.2 0.2 fusion.12
  130.5 0.6 collective-permute-done.15
  131.1 5.6 %collective-permute-start.16 = (bf16[2,64,128]{2,1,0:T(8,128)(2,1)S(1)}, bf16[2,64,128]{2,1,0:T(8,128)(2,1)S(1)}, u32[]{:S(2)}, u32[]{:S(2)}) collective-permute-start(bf16[2,64,128]{2,1,0:T(8,128)(2,1)S(1)} %collective-permute-done.14), channel_id=1, source_target_pairs={{0,30},{2,0},{4,2},{6,4},{8,6},{10,8},{12,10},{14,12},{16,14},{18,... | collective-permute-start | bytes 98312 | tf_op jit(solution)/shard_map/ppermute | solution.py:20
  137.0 0.2 fusion.11
  137.2 1.4 collective-permute-done.17
  139.1 7.0 %collective-permute-done.18 = bf16[2,64,128]{2,1,0:T(8,128)(2,1)S(1)} collective-permute-done((bf16[2,64,128]{2,1,0:T(8,128)(2,1)S(1)}, bf16[2,64,128]{2,1,0:T(8,128)(2,1)S(1)}, u32[]{:S(2)}, u32[]{:S(2)}) %collective-permute-start.18) | collective-permute-done | bytes 32800 | tf_op jit(solution)/shard_map/ppermute | solution.py:18
  146.4 1.2 fusion.18
  147.7 1.2 convolution_bitcast_fusion.1
  149.1 1.9 fusion.9
  151.1 1.7 pad_maximum_fusion
  152.7 6.6 %gather_fusion = bf16[128,256,128]{2,1,0:T(8,128)(2,1)} fusion(bf16[32,256,128]{2,1,0:T(8,128)(2,1)S(1)} %bitcast.97, s32[1024]{0:T(1024)S(1)} %pad_clamp_fusion.2), kind=kCustom, calls=%fused_computation | custom fusion | bytes 16777728 | tf_op jit(solution)/shard_map/gather | solution.py:69
  159.3 12.1 %copy.58 = bf16[128,256,128]{1,2,0:T(8,128)(2,1)} copy(bf16[128,256,128]{2,1,0:T(8,128)(2,1)} %gather_fusion) | data formatting | bytes 16777216 | tf_op jit(solution)/shard_map/gather | solution.py:69
  171.4 12.7 %fusion.4 = f32[16,256,128]{1,2,0:T(8,128)} fusion(f32[16,128,256]{2,1,0:T(8,128)S(1)} %copy-done.2, bf16[16,8,256,256]{3,2,1,0:T(8,128)(2,1)} %all-gather.2.cloned.1.call-done, bf16[16,8,256,128]{2,3,1,0:T(8,128)(2,1)} %bitcast.99, pred[16,8]{1,0:T(8,128)(4,1)S(1)} %iota_compare_fusion.1), kind=kOutput, calls=%fused_computation.9 | convolution fusion | flops 2152202240 | bytes 29360256 | tf_op jit(solution)/shard_map/lsij,lsjc->lic/dot_general | solution.py:72
  184.1 2.9 %copy.81 = f32[16,256,128]{2,1,0:T(8,128)} copy(f32[16,256,128]{1,2,0:T(8,128)} %fusion.4) | data formatting | bytes 4194304 | tf_op jit(solution)/shard_map/add | solution.py:133
  (74 shorter events, 4.1 us)
Async XLA Ops:
  6.5 1.0 copy-start
  6.5 1.4 copy-start.1
  6.5 1.7 copy-start.4
  6.5 1.9 copy-start.7
  6.5 164.9 %all-gather.2.cloned.1.call-start = ((), (), s32[]{:S(2)}) async-start(), calls=%async_computation | async-start | bytes 25165824 | tf_op jit(solution)/shard_map/all_gather | solution.py:66
  7.3 17.3 %copy-start.12 = (s32[2,4]{1,0:T(2,128)S(1)}, s32[2,4]{1,0:T(2,128)}, u32[]{:S(2)}) copy-start(s32[2,4]{1,0:T(2,128)} %param.21) | copy-start | bytes 100
  7.3 17.4 %copy-start.10 = (s32[16,4]{0,1:T(4,128)S(1)}, s32[16,4]{0,1:T(4,128)}, u32[]{:S(2)}) copy-start(s32[16,4]{0,1:T(4,128)} %param.18) | copy-start | bytes 772
  7.3 17.5 %copy-start.9 = (s32[16,8]{0,1:T(8,128)S(1)}, s32[16,8]{0,1:T(8,128)}, u32[]{:S(2)}) copy-start(s32[16,8]{0,1:T(8,128)} %param.14) | copy-start | bytes 1540
  7.3 17.9 %copy-start.11 = (s32[16]{0:T(128)S(1)}, s32[16]{0:T(128)}, u32[]{:S(2)}) copy-start(s32[16]{0:T(128)} %param.15) | copy-start | bytes 196
  7.3 69.6 %copy-start.8 = (bf16[4,64,256]{2,1,0:T(8,128)(2,1)S(1)}, bf16[4,64,256]{2,1,0:T(8,128)(2,1)}, u32[]{:S(2)}) copy-start(bf16[4,64,256]{2,1,0:T(8,128)(2,1)} %param.23) | copy-start | bytes 393220
  8.6 69.5 %collective-permute-start.4 = (bf16[2,64,128]{2,1,0:T(8,128)(2,1)S(1)}, bf16[2,64,128]{2,1,0:T(8,128)(2,1)S(1)}, u32[]{:S(2)}, u32[]{:S(2)}) collective-permute-start(bf16[2,64,128]{2,1,0:T(8,128)(2,1)S(1)} %fusion.19), channel_id=1, source_target_pairs={{0,30},{2,0},{4,2},{6,4},{8,6},{10,8},{12,10},{14,12},{16,14},{18,... | collective-permute-start | bytes 98312 | tf_op jit(solution)/shard_map/ppermute | solution.py:20
  15.5 63.9 %collective-permute-start.5 = (bf16[2,64,128]{2,1,0:T(8,128)(2,1)S(1)}, bf16[2,64,128]{2,1,0:T(8,128)(2,1)S(1)}, u32[]{:S(2)}, u32[]{:S(2)}) collective-permute-start(bf16[2,64,128]{2,1,0:T(8,128)(2,1)S(1)} %fusion.19), channel_id=1, source_target_pairs={{0,2},{2,4},{4,6},{6,8},{8,10},{10,12},{12,14},{14,16},{16,18},{18... | collective-permute-start | bytes 98312 | tf_op jit(solution)/shard_map/ppermute | solution.py:18
  15.6 100.3 %collective-permute-start.2 = (bf16[8,64,128]{2,1,0:T(8,128)(2,1)S(1)}, bf16[8,64,128]{2,1,0:T(8,128)(2,1)S(1)}, u32[]{:S(2)}, u32[]{:S(2)}) collective-permute-start(bf16[8,64,128]{2,1,0:T(8,128)(2,1)S(1)} %get-tuple-element.7), channel_id=1, source_target_pairs={{0,2},{2,4},{4,6},{6,8},{8,10},{10,12},{12,14},{14,16},{16,18},{18... | collective-permute-start | bytes 393224 | tf_op jit(solution)/shard_map/ppermute | solution.py:33
  16.9 104.7 %collective-permute-start.3 = (bf16[8,64,128]{2,1,0:T(8,128)(2,1)S(1)}, bf16[8,64,128]{2,1,0:T(8,128)(2,1)}, u32[]{:S(2)}, u32[]{:S(2)}) collective-permute-start(bf16[8,64,128]{2,1,0:T(8,128)(2,1)S(1)} %get-tuple-element.8), channel_id=1, source_target_pairs={{2,0},{4,2},{6,4},{8,6},{10,8},{12,10},{14,12},{16,14},{18,16},{20... | collective-permute-start | bytes 393224 | tf_op jit(solution)/shard_map/ppermute | solution.py:34
  19.2 131.8 %collective-permute-start = (bf16[2048,128]{1,0:T(8,128)(2,1)}, bf16[2048,128]{1,0:T(8,128)(2,1)}, u32[]{:S(2)}, u32[]{:S(2)}) collective-permute-start(bf16[2048,128]{1,0:T(8,128)(2,1)} %get-tuple-element.5), channel_id=1, source_target_pairs={{0,2},{2,4},{4,6},{6,8},{8,10},{10,12},{12,14},{14,16},{16,18},{18... | collective-permute-start | bytes 1572872 | tf_op jit(solution)/shard_map/ppermute | solution.py:33
  78.1 72.9 %collective-permute-start.1 = (bf16[2048,128]{1,0:T(8,128)(2,1)}, bf16[2048,128]{1,0:T(8,128)(2,1)}, u32[]{:S(2)}, u32[]{:S(2)}) collective-permute-start(bf16[2048,128]{1,0:T(8,128)(2,1)} %get-tuple-element.6), channel_id=1, source_target_pairs={{2,0},{4,2},{6,4},{8,6},{10,8},{12,10},{14,12},{16,14},{18,16},{20... | collective-permute-start | bytes 1572872 | tf_op jit(solution)/shard_map/ppermute | solution.py:34
  79.4 7.7 %collective-permute-start.7 = (bf16[2,64,128]{2,1,0:T(8,128)(2,1)S(1)}, bf16[2,64,128]{2,1,0:T(8,128)(2,1)S(1)}, u32[]{:S(2)}, u32[]{:S(2)}) collective-permute-start(bf16[2,64,128]{2,1,0:T(8,128)(2,1)S(1)} %collective-permute-done.5), channel_id=1, source_target_pairs={{0,2},{2,4},{4,6},{6,8},{8,10},{10,12},{12,14},{14,16},{16,18},{18... | collective-permute-start | bytes 98312 | tf_op jit(solution)/shard_map/ppermute | solution.py:18
  87.1 4.6 %collective-permute-start.6 = (bf16[2,64,128]{2,1,0:T(8,128)(2,1)S(1)}, bf16[2,64,128]{2,1,0:T(8,128)(2,1)S(1)}, u32[]{:S(2)}, u32[]{:S(2)}) collective-permute-start(bf16[2,64,128]{2,1,0:T(8,128)(2,1)S(1)} %collective-permute-done.4), channel_id=1, source_target_pairs={{0,30},{2,0},{4,2},{6,4},{8,6},{10,8},{12,10},{14,12},{16,14},{18,... | collective-permute-start | bytes 98312 | tf_op jit(solution)/shard_map/ppermute | solution.py:20
  91.8 7.5 %collective-permute-start.9 = (bf16[2,64,128]{2,1,0:T(8,128)(2,1)S(1)}, bf16[2,64,128]{2,1,0:T(8,128)(2,1)S(1)}, u32[]{:S(2)}, u32[]{:S(2)}) collective-permute-start(bf16[2,64,128]{2,1,0:T(8,128)(2,1)S(1)} %collective-permute-done.7), channel_id=1, source_target_pairs={{0,2},{2,4},{4,6},{6,8},{8,10},{10,12},{12,14},{14,16},{16,18},{18... | collective-permute-start | bytes 98312 | tf_op jit(solution)/shard_map/ppermute | solution.py:18
  99.3 3.9 %collective-permute-start.8 = (bf16[2,64,128]{2,1,0:T(8,128)(2,1)S(1)}, bf16[2,64,128]{2,1,0:T(8,128)(2,1)S(1)}, u32[]{:S(2)}, u32[]{:S(2)}) collective-permute-start(bf16[2,64,128]{2,1,0:T(8,128)(2,1)S(1)} %collective-permute-done.6), channel_id=1, source_target_pairs={{0,30},{2,0},{4,2},{6,4},{8,6},{10,8},{12,10},{14,12},{16,14},{18,... | collective-permute-start | bytes 98312 | tf_op jit(solution)/shard_map/ppermute | solution.py:20
  100.1 49.0 %copy-start.3 = (bf16[16,64,256]{2,1,0:T(8,128)(2,1)S(1)}, bf16[16,64,256]{2,1,0:T(8,128)(2,1)}, u32[]{:S(2)}) copy-start(bf16[16,64,256]{2,1,0:T(8,128)(2,1)} %param.17) | copy-start | bytes 1572868
  103.2 7.6 %collective-permute-start.11 = (bf16[2,64,128]{2,1,0:T(8,128)(2,1)S(1)}, bf16[2,64,128]{2,1,0:T(8,128)(2,1)}, u32[]{:S(2)}, u32[]{:S(2)}) collective-permute-start(bf16[2,64,128]{2,1,0:T(8,128)(2,1)S(1)} %collective-permute-done.9), channel_id=1, source_target_pairs={{0,2},{2,4},{4,6},{6,8},{8,10},{10,12},{12,14},{14,16},{16,18},{18... | collective-permute-start | bytes 98312 | tf_op jit(solution)/shard_map/ppermute | solution.py:18
  110.8 4.0 %collective-permute-start.10 = (bf16[2,64,128]{2,1,0:T(8,128)(2,1)S(1)}, bf16[2,64,128]{2,1,0:T(8,128)(2,1)}, u32[]{:S(2)}, u32[]{:S(2)}) collective-permute-start(bf16[2,64,128]{2,1,0:T(8,128)(2,1)S(1)} %collective-permute-done.8), channel_id=1, source_target_pairs={{0,30},{2,0},{4,2},{6,4},{8,6},{10,8},{12,10},{14,12},{16,14},{18,... | collective-permute-start | bytes 98312 | tf_op jit(solution)/shard_map/ppermute | solution.py:20
  114.8 8.5 %collective-permute-start.13 = (bf16[2,64,128]{2,1,0:T(8,128)(2,1)}, bf16[2,64,128]{2,1,0:T(8,128)(2,1)}, u32[]{:S(2)}, u32[]{:S(2)}) collective-permute-start(bf16[2,64,128]{2,1,0:T(8,128)(2,1)} %collective-permute-done.11), channel_id=1, source_target_pairs={{0,2},{2,4},{4,6},{6,8},{8,10},{10,12},{12,14},{14,16},{16,18},{18... | collective-permute-start | bytes 98312 | tf_op jit(solution)/shard_map/ppermute | solution.py:18
  115.8 5.7 %copy-start.6 = (bf16[8,64,128]{2,1,0:T(8,128)(2,1)}, bf16[8,64,128]{2,1,0:T(8,128)(2,1)S(1)}, u32[]{:S(2)}) copy-start(bf16[8,64,128]{2,1,0:T(8,128)(2,1)S(1)} %collective-permute-done.2) | copy-start | bytes 393220
  115.9 7.6 %collective-permute-start.12 = (bf16[2,64,128]{2,1,0:T(8,128)(2,1)}, bf16[2,64,128]{2,1,0:T(8,128)(2,1)S(1)}, u32[]{:S(2)}, u32[]{:S(2)}) collective-permute-start(bf16[2,64,128]{2,1,0:T(8,128)(2,1)} %collective-permute-done.10), channel_id=1, source_target_pairs={{0,30},{2,0},{4,2},{6,4},{8,6},{10,8},{12,10},{14,12},{16,14},{18,... | collective-permute-start | bytes 98312 | tf_op jit(solution)/shard_map/ppermute | solution.py:20
  122.6 25.1 %copy-start.5 = (bf16[8,64,128]{2,1,0:T(8,128)(2,1)S(1)}, bf16[8,64,128]{2,1,0:T(8,128)(2,1)}, u32[]{:S(2)}) copy-start(bf16[8,64,128]{2,1,0:T(8,128)(2,1)} %copy.61) | copy-start | bytes 393220
  123.3 7.8 %collective-permute-start.15 = (bf16[2,64,128]{2,1,0:T(8,128)(2,1)}, bf16[2,64,128]{2,1,0:T(8,128)(2,1)S(1)}, u32[]{:S(2)}, u32[]{:S(2)}) collective-permute-start(bf16[2,64,128]{2,1,0:T(8,128)(2,1)} %collective-permute-done.13), channel_id=1, source_target_pairs={{0,2},{2,4},{4,6},{6,8},{8,10},{10,12},{12,14},{14,16},{16,18},{18... | collective-permute-start | bytes 98312 | tf_op jit(solution)/shard_map/ppermute | solution.py:18
  123.4 7.7 %collective-permute-start.14 = (bf16[2,64,128]{2,1,0:T(8,128)(2,1)S(1)}, bf16[2,64,128]{2,1,0:T(8,128)(2,1)S(1)}, u32[]{:S(2)}, u32[]{:S(2)}) collective-permute-start(bf16[2,64,128]{2,1,0:T(8,128)(2,1)S(1)} %collective-permute-done.12), channel_id=1, source_target_pairs={{0,30},{2,0},{4,2},{6,4},{8,6},{10,8},{12,10},{14,12},{16,14},{18,... | collective-permute-start | bytes 98312 | tf_op jit(solution)/shard_map/ppermute | solution.py:20
  131.1 7.5 %collective-permute-start.17 = (bf16[2,64,128]{2,1,0:T(8,128)(2,1)S(1)}, bf16[2,64,128]{2,1,0:T(8,128)(2,1)S(1)}, u32[]{:S(2)}, u32[]{:S(2)}) collective-permute-start(bf16[2,64,128]{2,1,0:T(8,128)(2,1)S(1)} %collective-permute-done.15), channel_id=1, source_target_pairs={{0,2},{2,4},{4,6},{6,8},{8,10},{10,12},{12,14},{14,16},{16,18},{18... | collective-permute-start | bytes 98312 | tf_op jit(solution)/shard_map/ppermute | solution.py:18
  131.1 7.7 %collective-permute-start.16 = (bf16[2,64,128]{2,1,0:T(8,128)(2,1)S(1)}, bf16[2,64,128]{2,1,0:T(8,128)(2,1)S(1)}, u32[]{:S(2)}, u32[]{:S(2)}) collective-permute-start(bf16[2,64,128]{2,1,0:T(8,128)(2,1)S(1)} %collective-permute-done.14), channel_id=1, source_target_pairs={{0,30},{2,0},{4,2},{6,4},{8,6},{10,8},{12,10},{14,12},{16,14},{18,... | collective-permute-start | bytes 98312 | tf_op jit(solution)/shard_map/ppermute | solution.py:20
  138.6 7.5 %collective-permute-start.18 = (bf16[2,64,128]{2,1,0:T(8,128)(2,1)S(1)}, bf16[2,64,128]{2,1,0:T(8,128)(2,1)S(1)}, u32[]{:S(2)}, u32[]{:S(2)}) collective-permute-start(bf16[2,64,128]{2,1,0:T(8,128)(2,1)S(1)} %collective-permute-done.17), channel_id=1, source_target_pairs={{0,2},{2,4},{4,6},{6,8},{8,10},{10,12},{12,14},{14,16},{16,18},{18... | collective-permute-start | bytes 98312 | tf_op jit(solution)/shard_map/ppermute | solution.py:18
  159.3 12.1 %copy-start.2 = (f32[16,128,256]{2,1,0:T(8,128)S(1)}, f32[16,128,256]{2,1,0:T(8,128)}, u32[]{:S(2)}) copy-start(f32[16,128,256]{2,1,0:T(8,128)} %fusion.9) | copy-start | bytes 6291460
Sparse Core Ops, SparseCore 0:
  8.9 32.7 all-gather.1
